TPU v7x, 32 devices: a whole 2x2x4 slice. The times are simulated.
32 devices in a mesh: ctx: 16 (over z, y, core), kvh: 2 (over x).
Axes of the slice: x: 2, y: 2, z: 4, core: 2. Of those that a mesh axis runs over, the one named last changes fastest.
Arguments:
- queries: bfloat16 [4096, 2048], P(('ctx', 'kvh')), may hold values from -6 to 6
- keys: bfloat16 [4096, 256], P(('ctx', 'kvh')), may hold values from -8 to 8
- values: bfloat16 [4096, 256], P(('ctx', 'kvh')), may hold values from -6 to 6
- grad_out: bfloat16 [4096, 2048], P(('ctx', 'kvh')), may hold values from -6 to 6
- doc_lengths: int32 [8], replicated, may hold values from 1 to 1024, 4096 in all
Outputs:
- attended: bfloat16 [4096, 2048], P(('ctx', 'kvh'))
- grad_queries: bfloat16 [4096, 2048], P(('ctx', 'kvh'))
- grad_keys: bfloat16 [4096, 256], P(('ctx', 'kvh'))
- grad_values: bfloat16 [4096, 256], P(('ctx', 'kvh'))
Inputs may be any that keep to these rules, and one draw needn't show every extreme that they name: `doc_lengths`: 8 lengths that sum to 4096; the longest is exactly 1024.
All inputs are finite; a program needn't handle non-finite values.
Results may differ from a plain program's by a relative error of at most 0.0076.
Values may be sent and summed in bfloat16 or wider, within the bound.
A program may use at most 64 MiB of HBM per device.

v0:
```python
import functools
import math

import jax
import jax.numpy as jnp
from jax import lax
from jax.experimental import pallas as pl
from jax.experimental.pallas import tpu as pltpu
from jax.sharding import PartitionSpec as P

REACH = 4
LANES = 256
SPAN = 3
NEG_LARGE = -1e30
F32 = jnp.float32
BF16 = jnp.bfloat16
MESH = pl.DeviceIdType.MESH


def matmul(a, b):
    return lax.dot_general(a, b, (((1,), (0,)), ((), ())), preferred_element_type=F32)


def kernel(
    ranges, groups, head_width, doc_ref, q_hbm, k_hbm, v_hbm, do_hbm,
    att_ref, gq_ref, gk_out, gv_out,
    q_ref, do_ref, kv_ref, kvt_ref, bias_ref, s_bufs, e_bufs, acc_ref, out_ref, in_ref, pair_ref, prior_ref, gk_ref, gv_ref,
    load_sem, kv_send, kv_recv, pass_send, back_send, back_recv, pair_recv,
):
    tokens = q_ref.shape[0]
    reach = REACH * groups
    slots = reach + 1
    window = slots * tokens
    heads = q_ref.shape[1] // head_width // groups
    per_step = LANES // tokens
    spans = [
        pl.ds(a * tokens, min(SPAN, slots - a) * tokens) for a in range(0, slots, SPAN)
    ]
    steps = heads // per_step
    blocks = ranges * groups
    scale = 1.0 / math.sqrt(head_width)
    scale_2 = scale * math.log2(math.e)
    me = lax.axis_index("ctx") * groups + lax.axis_index("kvh")

    place = me % reach
    band = me - place
    core = (place // groups) % 2
    chip = place - core * groups
    toward_partner = groups * (1 - 2 * core)

    def device(block):
        return (block // groups, block % groups)

    def both(*conditions):
        held = conditions[0]
        for condition in conditions[1:]:
            held = jnp.logical_and(held, condition)
        return held

    def core_of(at):
        return (at // groups) % 2

    def chip_of(at):
        return at - core_of(at) * groups

    def shared(source, at):
        first = chip_of(at)
        return both(
            chip_of(source) != first,
            jnp.logical_or(source < first, source > first + groups),
        )

    def reached(d):
        target = (place + d) % reach
        relayed = both(core_of(target) != core, shared(place, target))
        own = place + d < reach
        exists = jnp.logical_or(own, band > 0)
        return target, own, both(exists, jnp.logical_not(relayed))

    def source_of(d):
        source = (place - d + reach) % reach
        exists = me - d >= 0
        pair = both(exists, shared(source, place))
        same = core_of(source) == core
        return source, exists, both(pair, same), both(pair, jnp.logical_not(same))

    def slot(s):
        return pl.ds(s * tokens, tokens)

    own_loads = []
    for g in range(groups):
        columns = pl.ds(g * head_width, head_width)
        for i, src in enumerate((k_hbm, v_hbm)):
            own_loads.append(
                pltpu.make_async_copy(
                    src.at[:, columns],
                    kv_ref.at[g, slot(reach), pl.ds(i * head_width, head_width)],
                    load_sem.at[2 * g + i],
                )
            )
    big_loads = [
        pltpu.make_async_copy(q_hbm, q_ref, load_sem.at[2 * groups]),
        pltpu.make_async_copy(do_hbm, do_ref, load_sem.at[2 * groups + 1]),
    ]
    for copy in own_loads + big_loads:
        copy.start()

    barrier = pltpu.get_barrier_semaphore()
    for d in range(1, reach):
        pl.semaphore_signal(
            barrier, 1, device_id=device(band + (place + d) % reach), device_id_type=MESH
        )
    has_next = me + reach < blocks
    has_prior = band > 0

    @pl.when(has_next)
    def _():
        pl.semaphore_signal(barrier, 1, device_id=device(me + reach), device_id_type=MESH)

    @pl.when(has_prior)
    def _():
        pl.semaphore_signal(barrier, 1, device_id=device(me - reach), device_id_type=MESH)

    def send(src, dst, send_sem, recv_sem, block):
        return pltpu.make_async_remote_copy(
            src_ref=src, dst_ref=dst, send_sem=send_sem, recv_sem=recv_sem,
            device_id=device(block), device_id_type=MESH,
        )

    def kv_copy(g, d, source_slot, block):
        return send(
            kv_ref.at[g, slot(source_slot), :], kv_ref.at[g, slot(reach - d), :],
            kv_send.at[g, d - 1], kv_recv.at[g, d - 1], block,
        )

    def kv_pass(g, d):
        other = d + toward_partner
        return send(
            kv_ref.at[g, slot(reach - d), :],
            kv_ref.at[g, pl.ds(pl.multiple_of((reach - other) * tokens, tokens), tokens), :],
            pass_send.at[g, d - 1], kv_recv.at[g, other - 1], me + toward_partner,
        )

    def back_pair(g, d):
        other = d + toward_partner
        return send(
            out_ref.at[g, slot(reach - d), :],
            pair_ref.at[g, pl.ds(pl.multiple_of((other - 1) * tokens, tokens), tokens), :],
            back_send.at[g, d - 1], pair_recv.at[g, other - 1], me + toward_partner,
        )

    def back_copy(g, d):
        block = me - reach if d == reach else band + (place - d + reach) % reach
        return send(
            out_ref.at[g, slot(reach - d), :], in_ref.at[g, slot(d - 1), :],
            back_send.at[g, d - 1], back_recv.at[g, d - 1], block,
        )

    pl.semaphore_wait(
        barrier, reach - 1 + jnp.where(has_next, 1, 0) + jnp.where(has_prior, 1, 0)
    )
    for copy in own_loads:
        copy.wait()
    for g in range(groups):

        @pl.when(has_next)
        def _():
            kv_copy(g, reach, reach, me + reach).start()

        for d in range(1, reach):
            target, own, straight = reached(d)

            @pl.when(both(own, straight))
            def _():
                kv_copy(g, d, reach, band + target).start()

    def forward_prior(g):
        @pl.when(has_prior)
        def _():
            kv_copy(g, reach, reach, me).wait_recv()

        for d in range(1, reach):
            target, own, straight = reached(d)

            @pl.when(both(jnp.logical_not(own), straight))
            def _():
                kv_copy(g, d, 0, band + target).start()

    def relay(g):
        for d in range(1, reach):
            _, _, relays, _ = source_of(d)

            @pl.when(relays)
            def _():
                kv_copy(g, d, reach, me).wait_recv()
                kv_pass(g, d).start()

    def receive(g):
        for d in range(1, reach):
            _, exists, relays, _ = source_of(d)

            @pl.when(both(exists, jnp.logical_not(relays)))
            def _():
                kv_copy(g, d, reach, me).wait_recv()

    def add_rows(target_ref, g, s, part_ref, rows):
        target_ref[g, slot(s), :] = (
            target_ref[g, slot(s), :].astype(F32) + part_ref[g, rows, :].astype(F32)
        ).astype(BF16)

    def send_partials(g):
        for d in range(1, reach):
            _, exists, relays, relayed = source_of(d)

            @pl.when(relayed)
            def _():
                back_pair(g, d).start()

            @pl.when(both(exists, jnp.logical_not(relays), jnp.logical_not(relayed)))
            def _():
                back_copy(g, d).start()

    def send_pair_sums(g):
        for d in range(1, reach):
            _, _, relays, _ = source_of(d)

            @pl.when(relays)
            def _():
                send(
                    out_ref.at[g, slot(reach - d), :], pair_ref.at[g, slot(d - 1), :],
                    back_send.at[g, d - 1], pair_recv.at[g, d - 1], me + toward_partner,
                ).wait_recv()
                add_rows(out_ref, g, reach - d, pair_ref, slot(d - 1))
                back_copy(g, d).start()

    def send_band_sums(g):
        for d in range(1, reach):
            _, own, straight = reached(d)

            @pl.when(both(jnp.logical_not(own), straight))
            def _():
                back_copy(g, d).wait_recv()
                part = in_ref[g, slot(d - 1), :].astype(F32)
                prior_ref[g] += part

        @pl.when(has_prior)
        def _():
            out_ref[g, slot(0), :] = prior_ref[g].astype(BF16)
            back_copy(g, reach).start()

    def collect(g):
        columns = slice(g * head_width, (g + 1) * head_width)

        def add(d):
            back_copy(g, d).wait_recv()
            part = in_ref[g, slot(d - 1), :].astype(F32)
            gk_ref[:, columns] += part[:, :head_width]
            gv_ref[:, columns] += part[:, head_width:]

        for d in range(1, reach):
            _, own, straight = reached(d)

            @pl.when(both(own, straight))
            def _():
                add(d)

        @pl.when(has_next)
        def _():
            add(reach)

    for d in range(1, reach + 1):

        @pl.when(me - d < 0)
        def _():
            for g in range(groups):
                kv_ref[g, slot(reach - d), :] = jnp.zeros((tokens, 2 * head_width), BF16)

    query_pos = me * tokens + lax.broadcasted_iota(jnp.int32, (8, LANES), 1) % tokens

    def next_doc(i, carry):
        start, first = carry
        first = jnp.where(start <= query_pos, jnp.maximum(first, start), first)
        return start + doc_ref[i], first

    _, doc_first = lax.fori_loop(
        0, doc_ref.shape[0], next_doc, (jnp.int32(0), jnp.zeros((8, LANES), jnp.int32))
    )
    for s in range(slots):
        key_pos = (me - reach + s) * tokens + lax.broadcasted_iota(jnp.int32, (tokens, LANES), 0)
        allowed = (key_pos >= doc_first[0:1]) & (key_pos <= query_pos[0:1])
        bias_ref[slot(s), :] = jnp.where(allowed, 0.0, NEG_LARGE)

    for copy in big_loads:
        copy.wait()

    forward_prior(0)
    relay(0)
    if groups > 1:
        forward_prior(1)

    for g in range(groups):
        receive(g)

        for s in range(slots):
            kvt_ref[:, slot(s)] = kv_ref[g, slot(s), :].T

        acc_ref[...] = jnp.zeros_like(acc_ref)

        def step(i, carry, s_ref, e_ref):
            first_head = g * heads + i * per_step

            def head_columns(j):
                return pl.ds((first_head + j) * head_width, head_width)

            def stacked(ref):
                return jnp.concatenate([ref[:, head_columns(j)] for j in range(per_step)], axis=0)

            q = stacked(q_ref)
            do = stacked(do_ref)
            q_t = q.T
            do_t = do.T
            top = jnp.full((8, LANES), NEG_LARGE, F32)
            for rows in spans:
                scores = matmul(kv_ref[g, rows, :head_width], q_t) * scale_2 + bias_ref[rows, :]
                s_ref[rows, :] = scores
                top = jnp.maximum(top, jnp.max(scores.reshape(-1, 8, LANES), axis=0))
            row_max = jnp.max(top, axis=0, keepdims=True)
            total = jnp.zeros((8, LANES), F32)
            for rows in spans:
                weights = jnp.exp2(s_ref[rows, :] - row_max)
                total = total + jnp.sum(weights.reshape(-1, 8, LANES), axis=0)
                e_ref[rows, :] = weights.astype(BF16)
            inverse = 1.0 / jnp.sum(total, axis=0, keepdims=True)
            out_t = (matmul(kvt_ref[head_width:, :], e_ref[...]) * inverse).astype(BF16)
            delta = jnp.sum(out_t.astype(F32) * do_t.astype(F32), axis=0, keepdims=True)
            out = out_t.T
            scaled_do = (do_t.astype(F32) * inverse).astype(BF16).T
            gq_t = jnp.zeros((head_width, LANES), F32)
            for rows in spans:
                weights = e_ref[rows, :]
                grad_probs = matmul(kv_ref[g, rows, head_width:], do_t)
                grad_scores = (weights.astype(F32) * ((grad_probs - delta) * inverse)).astype(BF16)
                gq_t = gq_t + matmul(kvt_ref[:head_width, rows], grad_scores)
                acc_ref[rows, :head_width] += matmul(grad_scores, q)
                acc_ref[rows, head_width:] += matmul(weights, scaled_do)
            gq = (gq_t * scale).astype(BF16).T
            for j in range(per_step):
                att_ref[:, head_columns(j)] = out[j * tokens:(j + 1) * tokens]
                gq_ref[:, head_columns(j)] = gq[j * tokens:(j + 1) * tokens]
            return carry

        for i in range(steps - 1):
            step(i, 0, s_bufs.at[i % 2], e_bufs.at[i % 2])
        if g + 1 < groups:
            relay(g + 1)
        if g + 2 < groups:
            forward_prior(g + 2)
        if g > 0:
            send_pair_sums(g - 1)
        step(steps - 1, 0, s_bufs.at[0], e_bufs.at[0])
        if g > 0:
            send_band_sums(g - 1)

        for d in range(1, reach):
            out_ref[g, slot(reach - d), :head_width] = (
                acc_ref[slot(reach - d), :head_width] * scale
            ).astype(BF16)
            out_ref[g, slot(reach - d), head_width:] = acc_ref[slot(reach - d), head_width:].astype(BF16)
        send_partials(g)
        prior_ref[g, :, :head_width] = acc_ref[slot(0), :head_width] * scale
        prior_ref[g, :, head_width:] = acc_ref[slot(0), head_width:]
        columns = slice(g * head_width, (g + 1) * head_width)
        gk_ref[:, columns] = acc_ref[slot(reach), :head_width] * scale
        gv_ref[:, columns] = acc_ref[slot(reach), head_width:]

    send_pair_sums(groups - 1)
    send_band_sums(groups - 1)
    for g in range(groups):
        collect(g)
    gk_out[...] = gk_ref[...].astype(BF16)
    gv_out[...] = gv_ref[...].astype(BF16)

    for g in range(groups):

        @pl.when(has_next)
        def _():
            kv_copy(g, reach, reach, me).wait_send()

        @pl.when(has_prior)
        def _():
            back_copy(g, reach).wait_send()

        for d in range(1, reach):
            _, _, straight = reached(d)
            _, exists, relays, _ = source_of(d)

            @pl.when(straight)
            def _():
                kv_copy(g, d, reach, me).wait_send()

            @pl.when(relays)
            def _():
                kv_pass(g, d).wait_send()

            @pl.when(exists)
            def _():
                back_copy(g, d).wait_send()


def on_device(ranges, groups, queries, keys, values, grad_out, doc_lengths):
    tokens = queries.shape[0]
    head_width = keys.shape[1] // groups
    reach = REACH * groups
    window = (reach + 1) * tokens
    anywhere = pl.BlockSpec(memory_space=pl.ANY)
    vmem = pl.BlockSpec(memory_space=pltpu.VMEM)
    dma = pltpu.SemaphoreType.DMA
    attended, grad_queries, grad_keys, grad_values = pl.pallas_call(
        functools.partial(kernel, ranges, groups, head_width),
        out_shape=(
            jax.ShapeDtypeStruct(queries.shape, BF16),
            jax.ShapeDtypeStruct(queries.shape, BF16),
            jax.ShapeDtypeStruct(keys.shape, BF16),
            jax.ShapeDtypeStruct(keys.shape, BF16),
        ),
        in_specs=[pl.BlockSpec(memory_space=pltpu.SMEM)] + [anywhere] * 4,
        out_specs=[vmem] * 4,
        scratch_shapes=[
            pltpu.VMEM(queries.shape, BF16),
            pltpu.VMEM(queries.shape, BF16),
            pltpu.VMEM((groups, window, 2 * head_width), BF16),
            pltpu.VMEM((2 * head_width, window), BF16),
            pltpu.VMEM((window, LANES), F32),
            pltpu.VMEM((2, window, LANES), F32),
            pltpu.VMEM((2, window, LANES), BF16),
            pltpu.VMEM((window, 2 * head_width), F32),
            pltpu.VMEM((groups, window, 2 * head_width), BF16),
            pltpu.VMEM((groups, reach * tokens, 2 * head_width), BF16),
            pltpu.VMEM((groups, reach * tokens, 2 * head_width), BF16),
            pltpu.VMEM((groups, tokens, 2 * head_width), F32),
            pltpu.VMEM(keys.shape, F32),
            pltpu.VMEM(keys.shape, F32),
            dma((2 * groups + 2,)),
            dma((groups, reach)),
            dma((groups, reach)),
            dma((groups, reach)),
            dma((groups, reach)),
            dma((groups, reach)),
            dma((groups, reach)),
        ],
        compiler_params=pltpu.CompilerParams(collective_id=0, has_side_effects=True),
    )(doc_lengths, queries, keys, values, grad_out)
    return attended, grad_queries, grad_keys, grad_values


def solution(mesh):
    rows = P(("ctx", "kvh"), None)
    return jax.shard_map(
        functools.partial(on_device, mesh.shape["ctx"], mesh.shape["kvh"]),
        mesh=mesh,
        in_specs=(rows, rows, rows, rows, P()),
        out_specs=(rows, rows, rows, rows),
        check_vma=False,
    )
```

profile of v0, /device:TPU:12, one launch (start us, length us, event | category | flops | bytes accessed | tf_op | source)
XLA Modules:
  0.0 42.2 jit_solution(11871039208471742050)
XLA Ops:
  0.6 37.3 %shard_map.84 = (bf16[128,2048]{1,0:T(8,128)(2,1)}, bf16[128,2048]{1,0:T(8,128)(2,1)}, bf16[128,256]{1,0:T(8,128)(2,1)}, bf16[128,256]{1,0:T(8,128)(2,1)}) custom-call(s32[8]{0:T(128)} %doc_ref.1, bf16[128,2048]{1,0:T(8,128)(2,1)} %q_hbm.1, bf16[128,256]{1,0:T(8,128)(2,1)} %k_hbm.1, bf16[128,256]{1,0:T(8,128)(2,1)} %v_hbm.1, bf16[128,2048]{1,0:T(8,128)(2,1)} %do_hbm.1), custom_call_target="tpu_custom_call" | custom-call | tf_op jit(solution)/shard_map/pallas_call | solution.py:418
  37.9 0.0 copy-start
  37.9 1.9 %copy.13 = bf16[128,2048]{1,0:T(8,128)(2,1)} copy(bf16[128,2048]{1,0:T(8,128)(2,1)} %get-tuple-element.8) | data formatting | bytes 1048576
  39.8 0.0 copy-done
  39.8 0.0 copy-start.2
  39.8 0.8 %copy.14 = bf16[128,2048]{1,0:T(8,128)(2,1)} copy(bf16[128,2048]{1,0:T(8,128)(2,1)S(1)} %copy-done) | data formatting | bytes 1048576
  40.6 0.1 copy-done.2
  40.7 0.0 copy-start.1
  40.7 0.6 %copy.15 = bf16[128,256]{1,0:T(8,128)(2,1)} copy(bf16[128,256]{1,0:T(8,128)(2,1)S(1)} %copy-done.2) | data formatting | bytes 131072
  41.3 0.2 copy-done.1
  41.6 0.6 %copy.16 = bf16[128,256]{1,0:T(8,128)(2,1)} copy(bf16[128,256]{1,0:T(8,128)(2,1)S(1)} %copy-done.1) | data formatting | bytes 131072
Async XLA Ops:
  37.9 2.0 %copy-start = (bf16[128,2048]{1,0:T(8,128)(2,1)S(1)}, bf16[128,2048]{1,0:T(8,128)(2,1)}, u32[]{:S(2)}) copy-start(bf16[128,2048]{1,0:T(8,128)(2,1)} %get-tuple-element.9) | copy-start | bytes 1572868
  39.8 0.9 %copy-start.2 = (bf16[128,256]{1,0:T(8,128)(2,1)S(1)}, bf16[128,256]{1,0:T(8,128)(2,1)}, u32[]{:S(2)}) copy-start(bf16[128,256]{1,0:T(8,128)(2,1)} %get-tuple-element.10) | copy-start | bytes 196612
  40.7 0.9 %copy-start.1 = (bf16[128,256]{1,0:T(8,128)(2,1)S(1)}, bf16[128,256]{1,0:T(8,128)(2,1)}, u32[]{:S(2)}) copy-start(bf16[128,256]{1,0:T(8,128)(2,1)} %get-tuple-element.11) | copy-start | bytes 196612
where the time goes:
time: 42.4 us; the launch traced here: 42.2 us
  Pallas kernels  37.3 us (88%)
  local copies, waits for them, and re-layouts  4.3 us (10%)
  between operations  0.65 us (2%)
    pallas_call x1, Pallas kernels, on_device(): pl.pallas_call(functools.partial(kernel, ranges, groups, head_width), out...  37.3 us
    unnamed x10, local copies, waits for them, and re-layouts  4.3 us

commit v1 on v0

v1 whole, which is shorter than its diff:
```python
import functools
import math

import jax
import jax.numpy as jnp
from jax import lax
from jax.experimental import pallas as pl
from jax.experimental.pallas import tpu as pltpu
from jax.sharding import PartitionSpec as P

REACH = 4
LANES = 256
CORES = 2
SPAN = 384
NEG_LARGE = -1e30
F32 = jnp.float32
BF16 = jnp.bfloat16
MESH = pl.DeviceIdType.MESH
K, V = 0, 1


def matmul(a, b):
    return lax.dot_general(a, b, (((1,), (0,)), ((), ())), preferred_element_type=F32)


def both(*conditions):
    held = conditions[0]
    for condition in conditions[1:]:
        held = jnp.logical_and(held, condition)
    return held


def kernel(
    ranges, groups, head_width, doc_hbm, q_hbm, k_hbm, v_hbm, do_hbm,
    att_ref, gq_ref, gk_out, gv_out,
    q_ref, do_ref, kv_ref, kvt_ref, oth_ref, bias_ref, s_ref, e_ref, inv_ref, sdo_ref, sdot_ref,
    attb_ref, gqb_ref, out_ref, back_ref, prior_ref, own_ref, zsum_ref, zin_ref, fin_ref, doc_ref,
    load_sem, qload_sem, doc_sem, xq_send, xq_recv, own_send, z_send, fwd_send, kv_recv,
    back_send, back_recv, zs_send, zin_recv, xo_send, xo_recv, lo_sem,
):
    tokens = gk_out.shape[0]
    reach = REACH * groups
    share = groups // CORES
    slots = reach + groups + 1
    rows = REACH // CORES
    chips = rows * groups
    width = q_ref.shape[2]
    heads = width // head_width // share
    per_step = LANES // tokens
    steps = heads // per_step
    blocks = ranges * groups
    scale = 1.0 / math.sqrt(head_width)
    scale_2 = scale * math.log2(math.e)
    window = (reach + 1) * tokens

    ctx = lax.axis_index("ctx")
    column = lax.axis_index("kvh")
    me = ctx * groups + column
    place = me % reach
    band = me - place
    core = ctx % CORES
    row = place // (CORES * groups)
    low = row * CORES * groups + column
    partner = me + groups * (1 - 2 * core)
    has_prior = band > 0
    has_next = band + reach < blocks
    others = [(r, x) for r in range(rows) for x in range(groups) if (r, x) != (0, 0)]

    def device(block):
        return (block // groups, block % groups)

    def slot(k):
        if isinstance(k, int):
            return pl.ds(k * tokens, tokens)
        return pl.ds(pl.multiple_of(k * tokens, tokens), tokens)

    def columns_at(i, size):
        return pl.ds(pl.multiple_of(i * size, size), size)

    def chip(r, x):
        r_t = (row + r) % rows
        x_t = (column + x) % groups
        return r_t, x_t, r_t * CORES * groups + x_t

    def exists(k):
        return jnp.logical_or(has_prior, k >= reach - low)

    def send(src, dst, send_sem, recv_sem, block):
        return pltpu.make_async_remote_copy(
            src_ref=src, dst_ref=dst, send_sem=send_sem, recv_sem=recv_sem,
            device_id=device(block), device_id_type=MESH,
        )

    own_slot = reach + core * groups

    loads = {}
    for t, src in enumerate((k_hbm, v_hbm)):
        for j in range(share):
            loads[t, j] = [
                pltpu.make_async_copy(
                    src.at[:, columns_at(core * share + j, head_width)],
                    kv_ref.at[t, j, slot(own_slot), :], load_sem.at[t, j, 0],
                ),
                pltpu.make_async_copy(
                    src.at[:, columns_at((1 - core) * share + j, head_width)],
                    oth_ref.at[t, j], load_sem.at[t, j, 1],
                ),
            ]
            for copy in loads[t, j]:
                copy.start()
    doc_load = pltpu.make_async_copy(doc_hbm, doc_ref, doc_sem)
    doc_load.start()
    q_loads = [
        pltpu.make_async_copy(src.at[:, columns_at(core, width)], dst.at[core], qload_sem.at[i])
        for i, (src, dst) in enumerate(((q_hbm, q_ref), (do_hbm, do_ref)))
    ]
    for copy in q_loads:
        copy.start()
    q_passes = [
        send(src.at[:, columns_at(1 - core, width)], dst.at[core], xq_send.at[i], xq_recv.at[i], partner)
        for i, (src, dst) in enumerate(((q_hbm, q_ref), (do_hbm, do_ref)))
    ]
    q_arrivals = [
        send(src.at[:, columns_at(1 - core, width)], dst.at[1 - core], xq_send.at[i], xq_recv.at[i], partner)
        for i, (src, dst) in enumerate(((q_hbm, q_ref), (do_hbm, do_ref)))
    ]

    barrier = pltpu.get_barrier_semaphore()

    def greet(block):
        pl.semaphore_signal(barrier, 1, device_id=device(block), device_id_type=MESH)

    for d in range(1, reach):
        greet(band + (place + d) % reach)
    for near, step_to in ((has_next, reach), (has_prior, -reach)):

        @pl.when(near)
        def _():
            for c in range(CORES):
                greet(band + step_to + low + c * groups)

    pl.semaphore_wait(
        barrier,
        reach - 1 + jnp.where(has_next, CORES, 0) + jnp.where(has_prior, CORES, 0),
    )

    def kv_copy(t, j, far, send_sem, k, block):
        src = oth_ref.at[t, j] if far else kv_ref.at[t, j, slot(own_slot), :]
        return send(src, kv_ref.at[t, j, slot(k), :], send_sem, kv_recv.at[t, j, k], block)

    def z_copy(t, j, far):
        c = 1 - core if far else core
        return kv_copy(t, j, far, z_send.at[t, j, far], core * groups, band + reach + low + c * groups)

    def partner_copy(t, j):
        return kv_copy(t, j, 1, own_send.at[t, j, 0, 1], own_slot, partner)

    def own_copy(t, j, i, far):
        r_t, x_t, low_t = chip(*others[i])
        c = 1 - core if far else core
        return place < low_t + groups, kv_copy(
            t, j, far, own_send.at[t, j, i + 1, far], place - low_t + reach,
            band + low_t + c * groups,
        )

    def prior_copy(t, j, which, i):
        r_t, x_t, low_t = chip(*others[i])
        s = low + which * groups
        k = s - low_t
        return both(has_prior, low_t < s), send(
            kv_ref.at[t, j, slot(which * groups), :], kv_ref.at[t, j, slot(k), :],
            fwd_send.at[t, j, which, i], kv_recv.at[t, j, k], band + low_t + core * groups,
        )

    def arrival(t, j, k):
        return send(
            oth_ref.at[t, j], kv_ref.at[t, j, slot(k), :], z_send.at[t, j, 0], kv_recv.at[t, j, k], partner
        )

    def send_down(t):
        for j in range(share):
            for copy in loads[t, j]:
                copy.wait()

            @pl.when(has_next)
            def _():
                z_copy(t, j, 0).start()
                z_copy(t, j, 1).start()

            partner_copy(t, j).start()

    def send_own(t):
        for j in range(share):
            for i in range(len(others)):
                for far in range(CORES):
                    needed, copy = own_copy(t, j, i, far)

                    @pl.when(needed)
                    def _():
                        copy.start()

    def send_prior(t):
        for j in range(share):
            for which in range(CORES):

                @pl.when(has_prior)
                def _():
                    arrival(t, j, which * groups).wait_recv()

                for i in range(len(others)):
                    needed, copy = prior_copy(t, j, which, i)

                    @pl.when(needed)
                    def _():
                        copy.start()

    def receive(t):
        for j in range(share):
            for k in range(slots):
                if k in (0, groups):
                    continue
                needed = exists(k)
                if k in (reach, reach + groups):
                    needed = core != (k - reach) // groups

                @pl.when(needed)
                def _():
                    arrival(t, j, k).wait_recv()

    send_down(K)
    send_own(K)
    send_down(V)
    for copy in q_passes:
        copy.start()

    for k in range(reach):

        @pl.when(jnp.logical_not(exists(k)))
        def _():
            for t in (K, V):
                for j in range(share):
                    kv_ref[t, j, slot(k), :] = jnp.zeros((tokens, head_width), BF16)

    doc_load.wait()
    for blk in range(CORES):
        first_block = band + low + blk * groups
        query_pos = first_block * tokens + lax.broadcasted_iota(jnp.int32, (8, LANES), 1) % tokens

        def next_doc(i, carry):
            start, first = carry
            first = jnp.where(start <= query_pos, jnp.maximum(first, start), first)
            return start + doc_ref[i], first

        _, doc_first = lax.fori_loop(
            0, doc_ref.shape[0], next_doc, (jnp.int32(0), jnp.zeros((8, LANES), jnp.int32))
        )
        for s in range(reach + 1):
            key_pos = (first_block - reach + s) * tokens + lax.broadcasted_iota(jnp.int32, (tokens, LANES), 0)
            allowed = (key_pos >= doc_first[0:1]) & (key_pos <= query_pos[0:1])
            bias_ref[blk, slot(s), :] = jnp.where(allowed, 0.0, NEG_LARGE)

    send_prior(K)
    send_own(V)
    send_prior(V)
    for copy in q_loads:
        copy.wait()
    for copy in q_arrivals:
        copy.wait_recv()
    receive(K)

    units = [(j, blk, i) for j in range(share) for blk in range(CORES) for i in range(steps)]

    def head_columns(j, i, n):
        return pl.ds((j * heads + i * per_step + n) * head_width, head_width)

    def stacked(ref, j, blk, i):
        return jnp.concatenate(
            [ref[blk, :, head_columns(j, i, n)] for n in range(per_step)], axis=0
        )

    spans = [pl.ds(a, min(SPAN, window - a)) for a in range(0, window, SPAN)]

    def window_rows(blk, rows_in):
        return pl.ds(blk * groups * tokens + rows_in.start, rows_in.size)

    for u, (j, blk, i) in enumerate(units):
        s_buf = s_ref.at[u % 2]
        q_t = stacked(q_ref, j, blk, i).T
        top = jnp.full((8, LANES), NEG_LARGE, F32)
        for span in spans:
            scores = matmul(kv_ref[K, j, window_rows(blk, span), :], q_t) * scale_2 + bias_ref[blk, span, :]
            s_buf[span, :] = scores
            top = jnp.maximum(top, jnp.max(scores.reshape(-1, 8, LANES), axis=0))
        row_max = jnp.max(top, axis=0, keepdims=True)
        total = jnp.zeros((8, LANES), F32)
        for span in spans:
            weights = jnp.exp2(s_buf[span, :] - row_max)
            total = total + jnp.sum(weights.reshape(-1, 8, LANES), axis=0)
            e_ref[j, blk, span, i * LANES:(i + 1) * LANES] = weights.astype(BF16)
        inverse = 1.0 / jnp.sum(total, axis=0, keepdims=True)
        inv_ref[u] = inverse
        scaled_t = (stacked(do_ref, j, blk, i).T.astype(F32) * inverse).astype(BF16)
        sdot_ref[u] = scaled_t
        sdo_ref[j, blk, i * LANES:(i + 1) * LANES, :] = scaled_t.T

    pieces = []
    most = max(1, 4 * 128 // tokens)
    for first, last, blks in (
        (0, groups, (0,)), (groups, reach + 1, (0, 1)), (reach + 1, slots, (1,)),
    ):
        for a in range(first, last, most):
            pieces.append((a, min(a + most, last), blks))

    def back_copy(t, j, k):
        own = k >= reach - low
        s = jnp.where(own, k - reach + low, k + low)
        r_s = s // (CORES * groups)
        c_s = (s // groups) % CORES
        x_s = s % groups
        block = band + jnp.where(own, s, s + (core - c_s) * groups)
        i = ((row - r_s + rows) % rows) * groups + (column - x_s + groups) % groups
        entry = jnp.where(
            own, i * groups + core * share + j, chips * groups + (c_s * chips + i) * share + j
        )
        return send(
            out_ref.at[t, j, slot(k), :], back_ref.at[t, entry],
            back_send.at[t, j, k], back_recv.at[t, entry], block,
        )

    def back_needed(k):
        if k in (reach, reach + groups):
            return core != (k - reach) // groups
        return exists(k)

    def partials(t, left_ref, right, factor):
        for j in range(share):
            for first, last, blks in pieces:
                total = None
                for blk in blks:
                    part = pl.ds((first - blk * groups) * tokens, (last - first) * tokens)
                    term = matmul(left_ref[j, blk, part, :], right[j, blk])
                    total = term if total is None else total + term
                if factor is not None:
                    total = total * factor
                for k in range(first, last):
                    mine = total[(k - first) * tokens:(k - first + 1) * tokens]
                    if k in (0, groups):
                        prior_ref[t, j, k // groups] = mine
                        continue
                    if k in (reach, reach + groups):
                        own_ref[t, j, (k - reach) // groups] = mine
                    out_ref[t, j, slot(k), :] = mine.astype(BF16)
                for k in range(first, last):
                    if k in (0, groups):
                        continue

                    @pl.when(back_needed(k))
                    def _():
                        back_copy(t, j, k).start()

    def landed(t, entry):
        return send(
            oth_ref.at[t, 0], back_ref.at[t, entry], z_send.at[t, 0, 0], back_recv.at[t, entry], partner
        )

    def z_back(t, j, which):
        return send(
            zsum_ref.at[t, j, which], zin_ref.at[t, core * share + j],
            zs_send.at[t, j, which], zin_recv.at[t, core * share + j],
            band - reach + low + which * groups,
        )

    def collect_prior(t):
        for j in range(share):
            for which in range(CORES):
                for i in range(len(others)):
                    r_t, x_t, low_t = chip(*others[i])
                    entry = chips * groups + (which * chips + i + 1) * share + j

                    @pl.when(both(has_prior, low_t < low + which * groups))
                    def _():
                        landed(t, entry).wait_recv()
                        prior_ref[t, j, which] += back_ref[t, entry].astype(F32)

                @pl.when(has_prior)
                def _():
                    zsum_ref[t, j, which] = prior_ref[t, j, which].astype(BF16)
                    z_back(t, j, which).start()

    def collect_own(t, out):
        for c in range(CORES):

            @pl.when(core == c)
            def _():
                for j in range(share):
                    at = c * share + j
                    out[:, at * head_width:(at + 1) * head_width] = own_ref[t, j, c]
                    at = (1 - c) * share + j
                    landed(t, at).wait_recv()
                    out[:, at * head_width:(at + 1) * head_width] = back_ref[t, at].astype(F32)

        for i in range(len(others)):
            r_t, x_t, low_t = chip(*others[i])

            @pl.when(place < low_t + groups)
            def _():
                for g in range(groups):
                    entry = (i + 1) * groups + g
                    landed(t, entry).wait_recv()
                    out[:, g * head_width:(g + 1) * head_width] += back_ref[t, entry].astype(F32)

    def collect_next(t, out):
        @pl.when(has_next)
        def _():
            for g in range(groups):
                send(
                    oth_ref.at[t, 0], zin_ref.at[t, g], z_send.at[t, 0, 0], zin_recv.at[t, g], partner
                ).wait_recv()
                out[:, g * head_width:(g + 1) * head_width] += zin_ref[t, g].astype(F32)

    scaled = {(j, blk): sdo_ref[j, blk] for j in range(share) for blk in range(CORES)}
    partials(V, e_ref, scaled, None)

    receive(V)
    for j in range(share):
        for t in (K, V):
            for k in range(slots):
                kvt_ref[t, j, :, slot(k)] = kv_ref[t, j, slot(k), :].T

    for u, (j, blk, i) in enumerate(units):
        here = slice(i * LANES, (i + 1) * LANES)
        inverse = inv_ref[u]
        whole = pl.ds(blk * groups * tokens, window)
        out_t = (matmul(kvt_ref[V, j, :, whole], e_ref[j, blk, :, here]) * inverse).astype(BF16)
        do_t = stacked(do_ref, j, blk, i).T.astype(F32)
        delta = jnp.sum(out_t.astype(F32) * do_t, axis=0, keepdims=True) * inverse
        out = out_t.T
        scaled_t = sdot_ref[u]
        gq_t = jnp.zeros((head_width, LANES), F32)
        for span in spans:
            grad_probs = matmul(kv_ref[V, j, window_rows(blk, span), :], scaled_t)
            grad_scores = e_ref[j, blk, span, here] * (grad_probs - delta).astype(BF16)
            e_ref[j, blk, span, here] = grad_scores
            gq_t = gq_t + matmul(kvt_ref[K, j, :, window_rows(blk, span)], grad_scores)
        gq = (gq_t * scale).astype(BF16).T
        for n in range(per_step):
            attb_ref[blk, :, head_columns(j, i, n)] = out[n * tokens:(n + 1) * tokens]
            gqb_ref[blk, :, head_columns(j, i, n)] = gq[n * tokens:(n + 1) * tokens]
        if u == len(units) // 2 - 1:
            collect_prior(V)

    def exchange(i, buf, out):
        return (
            pltpu.make_async_copy(buf.at[core], out.at[:, columns_at(core, width)], lo_sem.at[i]),
            send(
                buf.at[1 - core], out.at[:, columns_at(core, width)], xo_send.at[i], xo_recv.at[i], partner
            ),
            send(
                buf.at[1 - core], out.at[:, columns_at(1 - core, width)], xo_send.at[i], xo_recv.at[i], partner
            ),
        )

    outs = [exchange(0, attb_ref, att_ref), exchange(1, gqb_ref, gq_ref)]
    for local, away, _ in outs:
        away.start()
        local.start()

    asked = {
        (j, blk): jnp.concatenate([stacked(q_ref, j, blk, i) for i in range(steps)], axis=0)
        for j in range(share) for blk in range(CORES)
    }
    partials(K, e_ref, asked, scale)

    for t in (V, K):
        if t == V:
            collect_prior(K)
        collect_own(t, fin_ref.at[t])
        collect_next(t, fin_ref.at[t])
    gv_out[...] = fin_ref[V].astype(BF16)
    gk_out[...] = fin_ref[K].astype(BF16)

    for local, away, coming in outs:
        local.wait()
        coming.wait_recv()
        away.wait_send()
    for copy in q_passes:
        copy.wait_send()
    for t in (K, V):
        for j in range(share):
            partner_copy(t, j).wait_send()

            @pl.when(has_next)
            def _():
                z_copy(t, j, 0).wait_send()
                z_copy(t, j, 1).wait_send()

            for i in range(len(others)):
                for far in range(CORES):
                    needed, copy = own_copy(t, j, i, far)

                    @pl.when(needed)
                    def _():
                        copy.wait_send()

                for which in range(CORES):
                    needed, copy = prior_copy(t, j, which, i)

                    @pl.when(needed)
                    def _():
                        copy.wait_send()

            for k in range(slots):
                if k in (0, groups):
                    continue

                @pl.when(back_needed(k))
                def _():
                    back_copy(t, j, k).wait_send()

            @pl.when(has_prior)
            def _():
                z_back(t, j, 0).wait_send()
                z_back(t, j, 1).wait_send()


def finish(a, b, c, d, out_a, out_b, out_c, out_d, sem):
    copies = [
        pltpu.make_async_copy(src, dst, sem.at[i])
        for i, (src, dst) in enumerate(((a, out_a), (b, out_b), (c, out_c), (d, out_d)))
    ]
    for copy in copies:
        copy.start()
    for copy in copies:
        copy.wait()


def on_device(ranges, groups, queries, keys, values, grad_out, doc_lengths):
    tokens = queries.shape[0]
    head_width = keys.shape[1] // groups
    share = groups // CORES
    reach = REACH * groups
    slots = reach + groups + 1
    window = (reach + 1) * tokens
    chips = REACH // CORES * groups
    width = queries.shape[1] // CORES
    per_step = LANES // tokens
    steps = queries.shape[1] // groups // head_width // per_step
    units = share * CORES * steps
    anywhere = pl.BlockSpec(memory_space=pl.ANY)
    vmem = pl.BlockSpec(memory_space=pltpu.VMEM)
    dma = pltpu.SemaphoreType.DMA
    shapes = [queries.shape, queries.shape, keys.shape, keys.shape]
    results = pl.pallas_call(
        functools.partial(kernel, ranges, groups, head_width),
        out_shape=tuple(jax.ShapeDtypeStruct(shape, BF16) for shape in shapes),
        in_specs=[anywhere] * 5,
        out_specs=[vmem] * 4,
        scratch_shapes=[
            pltpu.VMEM((CORES, tokens, width), BF16),
            pltpu.VMEM((CORES, tokens, width), BF16),
            pltpu.VMEM((2, share, slots * tokens, head_width), BF16),
            pltpu.VMEM((2, share, head_width, slots * tokens), BF16),
            pltpu.VMEM((2, share, tokens, head_width), BF16),
            pltpu.VMEM((CORES, window, LANES), F32),
            pltpu.VMEM((2, window, LANES), F32),
            pltpu.VMEM((share, CORES, window, steps * LANES), BF16),
            pltpu.VMEM((units, 1, LANES), F32),
            pltpu.VMEM((share, CORES, steps * LANES, head_width), BF16),
            pltpu.VMEM((units, head_width, LANES), BF16),
            pltpu.VMEM((CORES, tokens, width), BF16),
            pltpu.VMEM((CORES, tokens, width), BF16),
            pltpu.VMEM((2, share, slots * tokens, head_width), BF16),
            pltpu.VMEM((2, 2 * chips * groups, tokens, head_width), BF16),
            pltpu.VMEM((2, share, CORES, tokens, head_width), F32),
            pltpu.VMEM((2, share, CORES, tokens, head_width), F32),
            pltpu.VMEM((2, share, CORES, tokens, head_width), BF16),
            pltpu.VMEM((2, groups, tokens, head_width), BF16),
            pltpu.VMEM((2, tokens, groups * head_width), F32),
            pltpu.SMEM(doc_lengths.shape, jnp.int32),
            dma((2, share, 2)),
            dma((2,)),
            dma,
            dma((2,)),
            dma((2,)),
            dma((2, share, chips, CORES)),
            dma((2, share, CORES)),
            dma((2, share, CORES, chips)),
            dma((2, share, slots)),
            dma((2, share, slots)),
            dma((2, 2 * chips * groups)),
            dma((2, share, CORES)),
            dma((2, groups)),
            dma((2,)),
            dma((2,)),
            dma((2,)),
        ],
        compiler_params=pltpu.CompilerParams(
            collective_id=0, has_side_effects=True, vmem_limit_bytes=40 * 1024 * 1024
        ),
    )(*[
        pltpu.with_memory_space_constraint(x, pltpu.HBM)
        for x in (doc_lengths, queries, keys, values, grad_out)
    ])
    return pl.pallas_call(
        finish,
        out_shape=tuple(jax.ShapeDtypeStruct(shape, BF16) for shape in shapes),
        in_specs=[anywhere] * 4,
        out_specs=[anywhere] * 4,
        scratch_shapes=[dma((4,))],
        compiler_params=pltpu.CompilerParams(vmem_limit_bytes=4 * 1024 * 1024),
    )(*results)


def solution(mesh):
    rows = P(("ctx", "kvh"), None)
    return jax.shard_map(
        functools.partial(on_device, mesh.shape["ctx"], mesh.shape["kvh"]),
        mesh=mesh,
        in_specs=(rows, rows, rows, rows, P()),
        out_specs=(rows, rows, rows, rows),
        check_vma=False,
    )
```

time: 42.4 us -> 34.3 us (0.81)
  local copies, waits for them, and re-layouts: 4.3 us -> 0 us
  Pallas kernels: 37.3 us -> 33.1 us
    pallas_call x1, Pallas kernels: 37.3 us -> 32.1 us  [on_device(): pl.pallas_call(functools.partial(kernel, ranges, groups, head_width), out...]
    unnamed x10 -> x0, local copies, waits for them, and re-layouts: 4.3 us -> none
    pallas_call x0 -> x1, Pallas kernels: none -> 1.03 us  [on_device(): pl.pallas_call(finish, out_shape=tuple((jax.ShapeDtypeStruct(shape, BF16)...]
where the time goes in v1:
time: 34.3 us; the launch traced here: 33.8 us
  Pallas kernels  33.1 us (97%)
  between operations  0.64 us (2%)
    pallas_call x1, Pallas kernels, on_device(): pl.pallas_call(functools.partial(kernel, ranges, groups, head_width), out...  32.1 us
    pallas_call x1, Pallas kernels, on_device(): pl.pallas_call(finish, out_shape=tuple((jax.ShapeDtypeStruct(shape, BF16)...  1.03 us

profile of v1, /device:TPU:12, one launch (start us, length us, event | category | flops | bytes accessed | tf_op | source)
XLA Modules:
  0.0 33.8 jit_solution(4829060627242639283)
XLA Ops:
  0.6 32.1 %shard_map.84 = (bf16[128,2048]{1,0:T(8,128)(2,1)S(1)}, bf16[128,2048]{1,0:T(8,128)(2,1)S(1)}, bf16[128,256]{1,0:T(8,128)(2,1)S(1)}, bf16[128,256]{1,0:T(8,128)(2,1)S(1)}) custom-call(s32[8]{0:T(128)} %doc_hbm.1, bf16[128,2048]{1,0:T(8,128)(2,1)} %q_hbm.1, bf16[128,256]{1,0:T(8,128)(2,1)} %k_hbm.1, bf16[128,256]{1,0:T(8,128)(2,1)} %v_hbm.1, ...), custom_call_target="tpu_custom_call" | custom-call | tf_op jit(solution)/shard_map/pallas_call | solution.py:553
  32.7 1.0 %shard_map.85 = (bf16[128,2048]{1,0:T(8,128)(2,1)}, bf16[128,2048]{1,0:T(8,128)(2,1)}, bf16[128,256]{1,0:T(8,128)(2,1)}, bf16[128,256]{1,0:T(8,128)(2,1)}) custom-call(bf16[128,2048]{1,0:T(8,128)(2,1)S(1)} %get-tuple-element.8.a, bf16[128,2048]{1,0:T(8,128)(2,1)S(1)} %get-tuple-element.9.b, bf16[128,256]{1,0:T(8,128)(2,1)S(1)} %get-tuple-element.10.c, ...), custom_call_target="tpu_custom_call" | custom-call | tf_op jit(solution)/shard_map/pallas_call | solution.py:604

commit v2 on v1

--- a/solution.py
+++ b/solution.py
@@ -11,7 +11,9 @@
 REACH = 4
 LANES = 256
 CORES = 2
-SPAN = 384
+SCORE_ROWS = 512
+GRAD_ROWS = 256
+AHEAD = 4
 NEG_LARGE = -1e30
 F32 = jnp.float32
 BF16 = jnp.bfloat16
@@ -33,9 +35,10 @@
 def kernel(
     ranges, groups, head_width, doc_hbm, q_hbm, k_hbm, v_hbm, do_hbm,
     att_ref, gq_ref, gk_out, gv_out,
-    q_ref, do_ref, kv_ref, kvt_ref, oth_ref, bias_ref, s_ref, e_ref, inv_ref, sdo_ref, sdot_ref,
+    q_ref, do_ref, kv_ref, kvt_ref, oth_ref, bias_ref, s_ref, e_ref, d_ref, qt_ref, dot_ref, acc_ref, max_ref, sum_ref, fac_ref, delta_ref,
+    sdo_ref, sdot_ref,
     attb_ref, gqb_ref, out_ref, back_ref, prior_ref, own_ref, zsum_ref, zin_ref, fin_ref, doc_ref,
-    load_sem, qload_sem, doc_sem, xq_send, xq_recv, own_send, z_send, fwd_send, kv_recv,
+    load_sem, qload_sem, doc_sem, xq_send, xq_recv, own_send, z_send, fwd_send, diag_send, band_sem, kv_recv,
     back_send, back_recv, zs_send, zin_recv, xo_send, xo_recv, lo_sem,
 ):
     tokens = gk_out.shape[0]
@@ -51,7 +54,6 @@
     blocks = ranges * groups
     scale = 1.0 / math.sqrt(head_width)
     scale_2 = scale * math.log2(math.e)
-    window = (reach + 1) * tokens
 
     ctx = lax.axis_index("ctx")
     column = lax.axis_index("kvh")
@@ -65,6 +67,8 @@
     has_prior = band > 0
     has_next = band + reach < blocks
     others = [(r, x) for r in range(rows) for x in range(groups) if (r, x) != (0, 0)]
+    aligned = [i for i, (r, x) in enumerate(others) if r == 0 or x == 0]
+    diagonal = [i for i in range(len(others)) if i not in aligned]
 
     def device(block):
         return (block // groups, block % groups)
@@ -144,6 +148,10 @@
         reach - 1 + jnp.where(has_next, CORES, 0) + jnp.where(has_prior, CORES, 0),
     )
 
+    @pl.when(has_prior)
+    def _():
+        pl.semaphore_signal(band_sem, 1, device_id=device(me - reach), device_id_type=MESH)
+
     def kv_copy(t, j, far, send_sem, k, block):
         src = oth_ref.at[t, j] if far else kv_ref.at[t, j, slot(own_slot), :]
         return send(src, kv_ref.at[t, j, slot(k), :], send_sem, kv_recv.at[t, j, k], block)
@@ -161,6 +169,13 @@
         return place < low_t + groups, kv_copy(
             t, j, far, own_send.at[t, j, i + 1, far], place - low_t + reach,
             band + low_t + c * groups,
+        )
+
+    def diagonal_copy(t, j, i, far):
+        r_t, x_t, low_t = chip(*others[i])
+        c = 1 - core if far else core
+        return both(has_next, low_t < place), kv_copy(
+            t, j, far, diag_send.at[t, j, i, far], place - low_t, band + reach + low_t + c * groups
         )
 
     def prior_copy(t, j, which, i):
@@ -201,22 +216,32 @@
 
     def send_prior(t):
         for j in range(share):
-            for which in range(CORES):
+            for which in (core, 1 - core):
 
                 @pl.when(has_prior)
                 def _():
                     arrival(t, j, which * groups).wait_recv()
 
-                for i in range(len(others)):
+                for i in aligned:
                     needed, copy = prior_copy(t, j, which, i)
 
                     @pl.when(needed)
                     def _():
                         copy.start()
 
-    def receive(t):
-        for j in range(share):
-            for k in range(slots):
+    def send_diagonal(t):
+        for j in range(share):
+            for i in diagonal:
+                for far in range(CORES):
+                    needed, copy = diagonal_copy(t, j, i, far)
+
+                    @pl.when(needed)
+                    def _():
+                        copy.start()
+
+    def receive(t, part):
+        for j in range(share):
+            for k in range(*part):
                 if k in (0, groups):
                     continue
                 needed = exists(k)
@@ -229,7 +254,14 @@
 
     send_down(K)
     send_own(K)
+
+    @pl.when(has_next)
+    def _():
+        pl.semaphore_wait(band_sem, 1)
+
+    send_diagonal(K)
     send_down(V)
+    send_diagonal(V)
     for copy in q_passes:
         copy.start()
 
@@ -266,9 +298,9 @@
         copy.wait()
     for copy in q_arrivals:
         copy.wait_recv()
-    receive(K)
-
     units = [(j, blk, i) for j in range(share) for blk in range(CORES) for i in range(steps)]
+    near, far_half, near_half = (reach, slots), (0, reach // 2), (reach // 2, reach)
+    parts = [near, far_half, near_half]
 
     def head_columns(j, i, n):
         return pl.ds((j * heads + i * per_step + n) * head_width, head_width)
@@ -278,38 +310,74 @@
             [ref[blk, :, head_columns(j, i, n)] for n in range(per_step)], axis=0
         )
 
-    spans = [pl.ds(a, min(SPAN, window - a)) for a in range(0, window, SPAN)]
-
-    def window_rows(blk, rows_in):
-        return pl.ds(blk * groups * tokens + rows_in.start, rows_in.size)
+    def cut(blk, part):
+        first = max(part[0], blk * groups)
+        last = min(part[1], blk * groups + reach + 1)
+        here = pl.ds(first * tokens, (last - first) * tokens)
+        return here, pl.ds((first - blk * groups) * tokens, (last - first) * tokens)
+
+    def chunks(rows_in, most):
+        return [(a, min(most, rows_in.size - a)) for a in range(0, rows_in.size, most)]
+
+    def lanes(i):
+        return slice(i * LANES, (i + 1) * LANES)
+
+    for r, part in enumerate(parts):
+        receive(K, part)
+        def scores_of(u):
+            j, blk, i = units[u]
+            s_buf = s_ref.at[u % 2]
+            here, there = cut(blk, part)
+            if r == 0:
+                qt_ref[u] = stacked(q_ref, j, blk, i).T
+            q_t = qt_ref[u]
+            top = jnp.full((8, LANES), NEG_LARGE, F32)
+            for a, n in chunks(here, SCORE_ROWS):
+                scores = (
+                    matmul(kv_ref[K, j, pl.ds(here.start + a, n), :], q_t) * scale_2
+                    + bias_ref[blk, pl.ds(there.start + a, n), :]
+                )
+                s_buf[pl.ds(a, n), :] = scores
+                top = jnp.maximum(top, jnp.max(scores.reshape(-1, 8, LANES), axis=0))
+            return jnp.max(top, axis=0, keepdims=True)
+
+        tops = [scores_of(0)]
+        for u, (j, blk, i) in enumerate(units):
+            s_buf = s_ref.at[u % 2]
+            here, there = cut(blk, part)
+            if u + 1 < len(units):
+                tops.append(scores_of(u + 1))
+            row_max = tops[u]
+            total = jnp.zeros((8, LANES), F32)
+            for a, n in chunks(here, SCORE_ROWS):
+                weights = jnp.exp2(s_buf[pl.ds(a, n), :] - row_max)
+                total = total + jnp.sum(weights.reshape(-1, 8, LANES), axis=0)
+                e_ref[j, blk, pl.ds(there.start + a, n), lanes(i)] = weights.astype(BF16)
+            max_ref[r, u] = row_max
+            sum_ref[r, u] = jnp.sum(total, axis=0, keepdims=True)
 
     for u, (j, blk, i) in enumerate(units):
-        s_buf = s_ref.at[u % 2]
-        q_t = stacked(q_ref, j, blk, i).T
-        top = jnp.full((8, LANES), NEG_LARGE, F32)
-        for span in spans:
-            scores = matmul(kv_ref[K, j, window_rows(blk, span), :], q_t) * scale_2 + bias_ref[blk, span, :]
-            s_buf[span, :] = scores
-            top = jnp.maximum(top, jnp.max(scores.reshape(-1, 8, LANES), axis=0))
-        row_max = jnp.max(top, axis=0, keepdims=True)
-        total = jnp.zeros((8, LANES), F32)
-        for span in spans:
-            weights = jnp.exp2(s_buf[span, :] - row_max)
-            total = total + jnp.sum(weights.reshape(-1, 8, LANES), axis=0)
-            e_ref[j, blk, span, i * LANES:(i + 1) * LANES] = weights.astype(BF16)
-        inverse = 1.0 / jnp.sum(total, axis=0, keepdims=True)
-        inv_ref[u] = inverse
-        scaled_t = (stacked(do_ref, j, blk, i).T.astype(F32) * inverse).astype(BF16)
-        sdot_ref[u] = scaled_t
-        sdo_ref[j, blk, i * LANES:(i + 1) * LANES, :] = scaled_t.T
-
-    pieces = []
-    most = max(1, 4 * 128 // tokens)
-    for first, last, blks in (
-        (0, groups, (0,)), (groups, reach + 1, (0, 1)), (reach + 1, slots, (1,)),
-    ):
-        for a in range(first, last, most):
-            pieces.append((a, min(a + most, last), blks))
+        row_max = jnp.maximum(jnp.maximum(max_ref[0, u], max_ref[1, u]), max_ref[2, u])
+        shares = [jnp.exp2(max_ref[r, u] - row_max) for r in range(len(parts))]
+        total = sum(shares[r] * sum_ref[r, u] for r in range(len(parts)))
+        inverse = 1.0 / total
+        do_t = stacked(do_ref, j, blk, i).T
+        dot_ref[u] = do_t
+        for r in range(len(parts)):
+            factor = shares[r] * inverse
+            fac_ref[r, u] = factor
+            scaled_t = (do_t.astype(F32) * factor).astype(BF16)
+            sdot_ref[r, u] = scaled_t
+            sdo_ref[r, j, blk, lanes(i), :] = scaled_t.T
+
+    most = max(1, 2 * 128 // tokens)
+
+    def pieces(part):
+        edges = [part[0]] + [k for k in (groups, reach + 1) if part[0] < k < part[1]] + [part[1]]
+        for first, last in zip(edges[:-1], edges[1:]):
+            blks = [blk for blk in range(CORES) if blk * groups <= first < blk * groups + reach + 1]
+            for a in range(first, last, most):
+                yield a, min(a + most, last), blks
 
     def back_copy(t, j, k):
         own = k >= reach - low
@@ -332,13 +400,13 @@
             return core != (k - reach) // groups
         return exists(k)
 
-    def partials(t, left_ref, right, factor):
-        for j in range(share):
-            for first, last, blks in pieces:
+    def partials(t, part, left_ref, right, factor):
+        for j in range(share):
+            for first, last, blks in pieces(part):
                 total = None
                 for blk in blks:
-                    part = pl.ds((first - blk * groups) * tokens, (last - first) * tokens)
-                    term = matmul(left_ref[j, blk, part, :], right[j, blk])
+                    there = pl.ds((first - blk * groups) * tokens, (last - first) * tokens)
+                    term = matmul(left_ref[j, blk, there, :], right(j, blk))
                     total = term if total is None else total + term
                 if factor is not None:
                     total = total * factor
@@ -350,13 +418,16 @@
                     if k in (reach, reach + groups):
                         own_ref[t, j, (k - reach) // groups] = mine
                     out_ref[t, j, slot(k), :] = mine.astype(BF16)
-                for k in range(first, last):
-                    if k in (0, groups):
-                        continue
-
-                    @pl.when(back_needed(k))
-                    def _():
-                        back_copy(t, j, k).start()
+
+    def send_partials(t, part):
+        for j in range(share):
+            for k in range(*part):
+                if k in (0, groups):
+                    continue
+
+                @pl.when(back_needed(k))
+                def _():
+                    back_copy(t, j, k).start()
 
     def landed(t, entry):
         return send(
@@ -417,37 +488,6 @@
                     oth_ref.at[t, 0], zin_ref.at[t, g], z_send.at[t, 0, 0], zin_recv.at[t, g], partner
                 ).wait_recv()
                 out[:, g * head_width:(g + 1) * head_width] += zin_ref[t, g].astype(F32)
-
-    scaled = {(j, blk): sdo_ref[j, blk] for j in range(share) for blk in range(CORES)}
-    partials(V, e_ref, scaled, None)
-
-    receive(V)
-    for j in range(share):
-        for t in (K, V):
-            for k in range(slots):
-                kvt_ref[t, j, :, slot(k)] = kv_ref[t, j, slot(k), :].T
-
-    for u, (j, blk, i) in enumerate(units):
-        here = slice(i * LANES, (i + 1) * LANES)
-        inverse = inv_ref[u]
-        whole = pl.ds(blk * groups * tokens, window)
-        out_t = (matmul(kvt_ref[V, j, :, whole], e_ref[j, blk, :, here]) * inverse).astype(BF16)
-        do_t = stacked(do_ref, j, blk, i).T.astype(F32)
-        delta = jnp.sum(out_t.astype(F32) * do_t, axis=0, keepdims=True) * inverse
-        out = out_t.T
-        scaled_t = sdot_ref[u]
-        gq_t = jnp.zeros((head_width, LANES), F32)
-        for span in spans:
-            grad_probs = matmul(kv_ref[V, j, window_rows(blk, span), :], scaled_t)
-            grad_scores = e_ref[j, blk, span, here] * (grad_probs - delta).astype(BF16)
-            e_ref[j, blk, span, here] = grad_scores
-            gq_t = gq_t + matmul(kvt_ref[K, j, :, window_rows(blk, span)], grad_scores)
-        gq = (gq_t * scale).astype(BF16).T
-        for n in range(per_step):
-            attb_ref[blk, :, head_columns(j, i, n)] = out[n * tokens:(n + 1) * tokens]
-            gqb_ref[blk, :, head_columns(j, i, n)] = gq[n * tokens:(n + 1) * tokens]
-        if u == len(units) // 2 - 1:
-            collect_prior(V)
 
     def exchange(i, buf, out):
         return (
@@ -461,54 +501,134 @@
         )
 
     outs = [exchange(0, attb_ref, att_ref), exchange(1, gqb_ref, gq_ref)]
-    for local, away, _ in outs:
+    order = [1, 2, 0]
+
+    def start_out(i):
+        local, away, _ = outs[i]
         away.start()
         local.start()
 
-    asked = {
-        (j, blk): jnp.concatenate([stacked(q_ref, j, blk, i) for i in range(steps)], axis=0)
-        for j in range(share) for blk in range(CORES)
-    }
-    partials(K, e_ref, asked, scale)
-
-    for t in (V, K):
-        if t == V:
-            collect_prior(K)
-        collect_own(t, fin_ref.at[t])
-        collect_next(t, fin_ref.at[t])
-    gv_out[...] = fin_ref[V].astype(BF16)
-    gk_out[...] = fin_ref[K].astype(BF16)
+    def value_gradients(r):
+        partials(V, parts[r], e_ref, lambda j, blk: sdo_ref[r, j, blk], None)
+
+    for r in order:
+        value_gradients(r)
+    for r in order:
+        send_partials(V, parts[r])
+
+    for r, part in enumerate(parts):
+        receive(V, part)
+        for j in range(share):
+            for k in range(*part):
+                kvt_ref[V, j, :, slot(k)] = kv_ref[V, j, slot(k), :].T
+        def outputs_of(u):
+            j, blk, i = units[u]
+            here, there = cut(blk, part)
+            return matmul(kvt_ref[V, j, :, here], e_ref[j, blk, there, lanes(i)])
+
+        ahead = [outputs_of(u) for u in range(AHEAD)]
+        for u, (j, blk, i) in enumerate(units):
+            if u + AHEAD < len(units):
+                ahead.append(outputs_of(u + AHEAD))
+            term = ahead[u] * fac_ref[r, u]
+            if r == 0:
+                acc_ref[u] = term
+            elif r < len(parts) - 1:
+                acc_ref[u] += term
+            else:
+                out_t = (acc_ref[u] + term).astype(BF16)
+                delta_ref[u] = jnp.sum(
+                    out_t.astype(F32) * dot_ref[u].astype(F32), axis=0, keepdims=True
+                )
+                out = out_t.T
+                for n in range(per_step):
+                    attb_ref[blk, :, head_columns(j, i, n)] = out[n * tokens:(n + 1) * tokens]
+    start_out(0)
+    for j in range(share):
+        for k in range(slots):
+            kvt_ref[K, j, :, slot(k)] = kv_ref[K, j, slot(k), :].T
+
+    def asked(j, blk):
+        return jnp.concatenate([stacked(q_ref, j, blk, i) for i in range(steps)], axis=0)
+
+    for at, r in enumerate(order):
+        part = parts[r]
+        items = []
+        for u, (j, blk, i) in enumerate(units):
+            here, there = cut(blk, part)
+            for a, n in chunks(here, GRAD_ROWS):
+                items.append((u, pl.ds(here.start + a, n), pl.ds(there.start + a, n), a == 0, a + n == here.size))
+
+        def probs(item):
+            u, mine, _, _, _ = item
+            return matmul(kv_ref[V, units[u][0], mine, :], sdot_ref[r, u])
+
+        ahead = [probs(item) for item in items[:AHEAD]]
+        for at_item, (u, mine, window_at, starts, ends) in enumerate(items):
+            j, blk, i = units[u]
+            if at_item + AHEAD < len(items):
+                ahead.append(probs(items[at_item + AHEAD]))
+            grad_probs = ahead[at_item]
+            ahead[at_item] = None
+            if starts:
+                delta = delta_ref[u] * fac_ref[r, u]
+                gq_t = jnp.zeros((head_width, LANES), F32) if at == 0 else acc_ref[u]
+            grad_scores = e_ref[j, blk, window_at, lanes(i)] * (grad_probs - delta).astype(BF16)
+            d_ref[j, blk, window_at, lanes(i)] = grad_scores
+            gq_t = gq_t + matmul(kvt_ref[K, j, :, mine], grad_scores)
+            if not ends:
+                continue
+            if at < len(order) - 1:
+                acc_ref[u] = gq_t
+            else:
+                gq = (gq_t * scale).astype(BF16).T
+                for n in range(per_step):
+                    gqb_ref[blk, :, head_columns(j, i, n)] = gq[n * tokens:(n + 1) * tokens]
+        partials(K, part, d_ref, asked, scale)
+        send_partials(K, part)
+        if at == 1:
+            collect_prior(V)
+    start_out(1)
+
+    collect_prior(K)
+
+    for copy in q_passes:
+        copy.wait_send()
+    for t in (K, V):
+        for j in range(share):
+            partner_copy(t, j).wait_send()
+
+            @pl.when(has_next)
+            def _():
+                z_copy(t, j, 0).wait_send()
+                z_copy(t, j, 1).wait_send()
+
+            for i in range(len(others)):
+                for far in range(CORES):
+                    needed, copy = own_copy(t, j, i, far)
+
+                    @pl.when(needed)
+                    def _():
+                        copy.wait_send()
+
+                if i in aligned:
+                    waits = [prior_copy(t, j, which, i) for which in range(CORES)]
+                else:
+                    waits = [diagonal_copy(t, j, i, far) for far in range(CORES)]
+                for needed, copy in waits:
+
+                    @pl.when(needed)
+                    def _():
+                        copy.wait_send()
 
     for local, away, coming in outs:
         local.wait()
         coming.wait_recv()
         away.wait_send()
-    for copy in q_passes:
-        copy.wait_send()
-    for t in (K, V):
-        for j in range(share):
-            partner_copy(t, j).wait_send()
-
-            @pl.when(has_next)
-            def _():
-                z_copy(t, j, 0).wait_send()
-                z_copy(t, j, 1).wait_send()
-
-            for i in range(len(others)):
-                for far in range(CORES):
-                    needed, copy = own_copy(t, j, i, far)
-
-                    @pl.when(needed)
-                    def _():
-                        copy.wait_send()
-
-                for which in range(CORES):
-                    needed, copy = prior_copy(t, j, which, i)
-
-                    @pl.when(needed)
-                    def _():
-                        copy.wait_send()
-
+    for t in (V, K):
+        collect_own(t, fin_ref.at[t])
+    for t in (V, K):
+        for j in range(share):
             for k in range(slots):
                 if k in (0, groups):
                     continue
@@ -516,6 +636,11 @@
                 @pl.when(back_needed(k))
                 def _():
                     back_copy(t, j, k).wait_send()
+
+    for t, result in ((V, gv_out), (K, gk_out)):
+        collect_next(t, fin_ref.at[t])
+        result[...] = fin_ref[t].astype(BF16)
+        for j in range(share):
 
             @pl.when(has_prior)
             def _():
@@ -562,11 +687,18 @@
             pltpu.VMEM((2, share, head_width, slots * tokens), BF16),
             pltpu.VMEM((2, share, tokens, head_width), BF16),
             pltpu.VMEM((CORES, window, LANES), F32),
-            pltpu.VMEM((2, window, LANES), F32),
+            pltpu.VMEM((2, reach // 2 * tokens, LANES), F32),
             pltpu.VMEM((share, CORES, window, steps * LANES), BF16),
+            pltpu.VMEM((share, CORES, window, steps * LANES), BF16),
+            pltpu.VMEM((units, head_width, LANES), BF16),
+            pltpu.VMEM((units, head_width, LANES), BF16),
+            pltpu.VMEM((units, head_width, LANES), F32),
+            pltpu.VMEM((3, units, 1, LANES), F32),
+            pltpu.VMEM((3, units, 1, LANES), F32),
+            pltpu.VMEM((3, units, 1, LANES), F32),
             pltpu.VMEM((units, 1, LANES), F32),
-            pltpu.VMEM((share, CORES, steps * LANES, head_width), BF16),
-            pltpu.VMEM((units, head_width, LANES), BF16),
+            pltpu.VMEM((3, share, CORES, steps * LANES, head_width), BF16),
+            pltpu.VMEM((3, units, head_width, LANES), BF16),
             pltpu.VMEM((CORES, tokens, width), BF16),
             pltpu.VMEM((CORES, tokens, width), BF16),
             pltpu.VMEM((2, share, slots * tokens, head_width), BF16),
@@ -585,6 +717,8 @@
             dma((2, share, chips, CORES)),
             dma((2, share, CORES)),
             dma((2, share, CORES, chips)),
+            dma((2, share, chips, CORES)),
+            pltpu.SemaphoreType.REGULAR,
             dma((2, share, slots)),
             dma((2, share, slots)),
             dma((2, 2 * chips * groups)),

time: 34.3 us -> 28.1 us (0.82)
  the two profiles are of different devices: /device:TPU:12 before, /device:TPU:21 now
where the time goes in v2:
time: 28.1 us; the launch traced here: 27.9 us
  Pallas kernels  27.3 us (97%)
  between operations  0.64 us (2%)
    pallas_call x1, Pallas kernels, on_device(): pl.pallas_call(functools.partial(kernel, ranges, groups, head_width), out...  26.2 us
    pallas_call x1, Pallas kernels, on_device(): pl.pallas_call(finish, out_shape=tuple((jax.ShapeDtypeStruct(shape, BF16)...  1.03 us

profile of v2, /device:TPU:21, one launch (start us, length us, event | category | flops | bytes accessed | tf_op | source)
XLA Modules:
  0.0 27.9 jit_solution(3972030870868929334)
XLA Ops:
  0.6 26.2 %shard_map.84 = (bf16[128,2048]{1,0:T(8,128)(2,1)S(1)}, bf16[128,2048]{1,0:T(8,128)(2,1)S(1)}, bf16[128,256]{1,0:T(8,128)(2,1)S(1)}, bf16[128,256]{1,0:T(8,128)(2,1)S(1)}) custom-call(s32[8]{0:T(128)} %doc_hbm.1, bf16[128,2048]{1,0:T(8,128)(2,1)} %q_hbm.1, bf16[128,256]{1,0:T(8,128)(2,1)} %k_hbm.1, bf16[128,256]{1,0:T(8,128)(2,1)} %v_hbm.1, ...), custom_call_target="tpu_custom_call" | custom-call | tf_op jit(solution)/shard_map/pallas_call | solution.py:678
  26.9 1.0 %shard_map.85 = (bf16[128,2048]{1,0:T(8,128)(2,1)}, bf16[128,2048]{1,0:T(8,128)(2,1)}, bf16[128,256]{1,0:T(8,128)(2,1)}, bf16[128,256]{1,0:T(8,128)(2,1)}) custom-call(bf16[128,2048]{1,0:T(8,128)(2,1)S(1)} %get-tuple-element.8.a, bf16[128,2048]{1,0:T(8,128)(2,1)S(1)} %get-tuple-element.9.b, bf16[128,256]{1,0:T(8,128)(2,1)S(1)} %get-tuple-element.10.c, ...), custom_call_target="tpu_custom_call" | custom-call | tf_op jit(solution)/shard_map/pallas_call | solution.py:738
